TPU v7x, 32 devices: a whole 2x2x4 slice. The times are simulated.
32 devices in a mesh: samples: 4 (over y, x), channel: 4 (over z), spatial: 2 (over core).
Axes of the slice: x: 2, y: 2, z: 4, core: 2. Of those that a mesh axis runs over, the one named last changes fastest.
Arguments:
- features: bfloat16 [512, 4, 2, 1024], P('channel', 'samples', 'spatial'), may hold values from -6 to 6
- conv_one: bfloat16 [27, 512, 512], P(None, 'channel'), may hold values from -0.0625 to 0.0625
- conv_two: bfloat16 [27, 512, 512], P(None, 'channel'), may hold values from -0.0625 to 0.0625
- cotangent: bfloat16 [512, 4, 2, 1024], P('channel', 'samples', 'spatial'), may hold values from -6 to 6
Outputs:
- mixed_out: bfloat16 [512, 4, 2, 1024], P('channel', 'samples', 'spatial')
- input_grad: bfloat16 [512, 4, 2, 1024], P('channel', 'samples', 'spatial')
- grad_one: float32 [27, 512, 512], P(None, 'channel')
- grad_two: float32 [27, 512, 512], P(None, 'channel')
All inputs are finite; a program needn't handle non-finite values.
Results may differ from a plain program's by a relative error of at most 0.017.
Values may be sent and summed in bfloat16 or wider, within the bound.
A program may use at most 128 MiB of HBM per device.

v0:
```python
import jax
import jax.numpy as jnp
from jax import lax
from jax.sharding import PartitionSpec as P

SIDE = 32


def with_halo(shard, sides, width):
    for axis, dim in sides:
        size, length = (lax.axis_size(axis), shard.shape[dim])
        up = [(i, (i + 1) % size) for i in range(size - 1)]
        down = [(j, i) for i, j in up]
        last = lax.slice_in_dim(shard, length - width, length, axis=dim)
        first = lax.slice_in_dim(shard, 0, width, axis=dim)
        before = lax.ppermute(last, axis, up)
        after = lax.ppermute(first, axis, down)
        shard = jnp.concatenate([before, shard, after], axis=dim)
    return shard


def to_grid(values):
    return values.reshape(values.shape[0], values.shape[1], values.shape[2], SIDE, SIDE)


def to_flat(values):
    return values.reshape(values.shape[0], values.shape[1], values.shape[2], SIDE * SIDE)


def as_taps(kernel):
    return kernel.reshape(3, 3, 3, kernel.shape[1], kernel.shape[2])


def forward_conv(source, kernel, rhs_spec):
    return lax.conv_general_dilated(
        source,
        as_taps(kernel),
        (1, 1, 1),
        [(0, 0), (1, 1), (1, 1)],
        dimension_numbers=("CNDHW", rhs_spec, "CNDHW"),
        preferred_element_type=jnp.float32,
    )


def data_grad(source, kernel, rhs_spec):
    flipped = as_taps(kernel)[::-1, ::-1, ::-1]
    return lax.conv_general_dilated(
        source,
        flipped,
        (1, 1, 1),
        [(0, 0), (1, 1), (1, 1)],
        dimension_numbers=("CNDHW", rhs_spec, "CNDHW"),
        preferred_element_type=jnp.float32,
    )


def weight_grad(padded, upstream, out_spec):
    result = lax.conv_general_dilated(
        padded,
        upstream,
        (1, 1, 1),
        [(0, 0), (0, 0), (0, 0)],
        dimension_numbers=("NCDHW", "OIDHW", out_spec),
        preferred_element_type=jnp.float32,
    )
    return result.reshape(27, result.shape[3], result.shape[4])


def pad_plane(values):
    return jnp.pad(values, ((0, 0), (0, 0), (0, 0), (1, 1), (1, 1)))


def body(features, conv_one, conv_two, cotangent):
    rims_x = with_halo(features, (("spatial", 2),), 1)
    whole_x = lax.all_gather(rims_x, "channel", axis=0, tiled=True)
    pre_act = forward_conv(to_grid(whole_x), conv_one, "DHWOI")
    hidden = jax.nn.silu(pre_act).astype(jnp.bfloat16)
    rims_h = with_halo(to_flat(hidden), (("spatial", 2),), 1)
    grid_h = to_grid(rims_h)
    weight_part = conv_two
    mixed_out = lax.psum_scatter(
        to_flat(forward_conv(grid_h, weight_part, "DHWIO")),
        "channel",
        scatter_dimension=0,
        tiled=True,
    ).astype(jnp.bfloat16)
    rims_c = with_halo(cotangent, (("spatial", 2),), 1)
    whole_c = to_grid(lax.all_gather(rims_c, "channel", axis=0, tiled=True))
    hidden_grad = data_grad(whole_c, conv_two, "DHWOI")
    sigmoid_v = jax.nn.sigmoid(pre_act)
    act_grad = (hidden_grad * sigmoid_v * (1.0 + pre_act * (1.0 - sigmoid_v))).astype(jnp.bfloat16)
    rims_g = with_halo(to_flat(act_grad), (("spatial", 2),), 1)
    grid_g = to_grid(rims_g)
    weight_part = conv_one
    input_grad = lax.psum_scatter(
        to_flat(data_grad(grid_g, weight_part, "DHWIO")).astype(jnp.bfloat16),
        "channel",
        scatter_dimension=0,
        tiled=True,
    )
    local_two = weight_grad(pad_plane(grid_h), whole_c[:, :, 1:-1], "DHWNC")
    local_one = weight_grad(pad_plane(to_grid(whole_x)), act_grad, "DHWCN")
    grad_one, grad_two = (
        lax.psum(local_one.astype(jnp.bfloat16), ("samples", "spatial")).astype(jnp.float32),
        lax.psum(local_two.astype(jnp.bfloat16), ("samples", "spatial")).astype(jnp.float32),
    )
    return (mixed_out, input_grad, grad_one, grad_two)


def solution(mesh):
    placed = (
        P("channel", "samples", "spatial", None),
        P(None, "channel", None),
        P(None, "channel", None),
        P("channel", "samples", "spatial", None),
    )
    return jax.shard_map(
        body,
        mesh=mesh,
        in_specs=placed,
        out_specs=(
            P("channel", "samples", "spatial", None),
            P("channel", "samples", "spatial", None),
            P(None, "channel", None),
            P(None, "channel", None),
        ),
        check_vma=False,
    )
```

profile of v0, /device:TPU:0, one launch (start us, length us, event | category | flops | bytes accessed | tf_op | source)
XLA Modules:
  0.0 412.6 jit_solution(8968176364339753036)
XLA Ops:
  7.2 1.9 copy.91
  9.2 2.4 collective-permute-start
  12.9 2.3 collective-permute-done.1
  19.0 2.0 collective-permute-start.4
  22.4 2.3 collective-permute-done.5
  24.7 1.9 pad_maximum_fusion.2
  26.7 56.1 %all-gather.3.cloned.1.call-done = bf16[512,1,3,1024]{0,3,2,1:T(8,128)(2,1)} async-done(((bf16[128,1,3,1024]{0,3,2,1:T(8,128)(2,1)}), bf16[512,1,3,1024]{0,3,2,1:T(8,128)(2,1)}) %all-gather.3.cloned.1.call-update) | async-done | bytes 3145744 | tf_op jit(solution)/shard_map/all_gather | solution.py:75
  82.8 3.6 copy.144
  88.0 2.2 copy.96
  90.7 10.3 %multiply_convert_fusion = (bf16[1,32,8,5,128]{4,2,3,1,0:T(8,128)(2,1)S(1)}, f32[1,32,8,5,128]{4,2,3,1,0:T(8,128)}) fusion(bf16[3,3,3,128,512]{4,3,2,1,0:T(8,128)(2,1)S(1)} %bitcast.81, bf16[512,3,32,1,7,2]{0,4,5,2,1,3:T(8,128)(2,1)S(1)} %slice.16, bf16[512,3,32,1,8,5]{0,4,5,2,1,3:T(8,128)(2,1)S(1)} %copy.96, pred[8,5]{0,1:T(8,128)(4,1)S(1)} %copy-done.15), kind=kOutput, calls=%fused_computation.63 | convolution fusion | flops 4452974592 | bytes 9830440 | tf_op jit(solution)/shard_map/conv_general_dilated | solution.py:35
  104.4 4.6 %collective-permute-start.2 = (bf16[128,1,1,1024]{0,3,2,1:T(8,128)(2,1)}, bf16[128,1,1,1024]{0,3,2,1:T(8,128)(2,1)}, u32[]{:S(2)}, u32[]{:S(2)}) collective-permute-start(bf16[128,1,1,1024]{0,3,2,1:T(8,128)(2,1)} %bitcast.42), channel_id=1, source_target_pairs={{0,1},{2,3},{4,5},{6,7},{8,9},{10,11},{12,13},{14,15},{16,17},{18,... | collective-permute-start | bytes 786440 | tf_op jit(solution)/shard_map/ppermute | solution.py:16
  110.3 3.5 fusion.83
  113.8 32.2 %all-gather.5.cloned.1.call-done = bf16[512,1,3,1024]{0,3,2,1:T(8,128)(2,1)} async-done(((bf16[128,1,3,1024]{0,3,2,1:T(8,128)(2,1)}), bf16[512,1,3,1024]{0,3,2,1:T(8,128)(2,1)}) %all-gather.5.cloned.1.call-update) | async-done | bytes 3145744 | tf_op jit(solution)/shard_map/all_gather | solution.py:88
  145.9 3.6 copy.147
  150.2 2.2 copy.111
  152.9 9.7 %fusion.57 = bf16[1,32,8,5,128]{4,2,3,1,0:T(8,128)(2,1)S(1)} fusion(bf16[3,3,3,128,512]{4,3,2,1,0:T(8,128)(2,1)S(1)} %bitcast.105, bf16[512,3,32,1,7,2]{0,4,5,2,1,3:T(8,128)(2,1)S(1)} %slice.20, bf16[512,3,32,1,8,5]{0,4,5,2,1,3:T(8,128)(2,1)S(1)} %copy.111, f32[1,32,8,5,128]{4,2,3,1,0:T(8,128)S(1)} %copy-done.17, pred[8,5]{0,1:T(8,128)(4,1)S(1)} %copy-done.15), kind=kOutput, calls=%fused_computation.54 | convolution fusion | flops 4453629952 | bytes 9830440 | tf_op jit(solution)/shard_map/conv_general_dilated | solution.py:47
  163.5 2.1 collective-permute-start.6
  171.3 2.2 copy.126
  175.1 15.5 %fusion.32 = bf16[3,3,3,128,512,1]{3,4,2,5,1,0:T(8,128)(2,1)} fusion(bf16[512,3,32,8,5,1]{0,3,5,4,2,1:T(8,128)(2,1)S(1)} %get-tuple-element.26, bf16[512,3,32,8,5,1]{0,3,5,4,2,1:T(8,128)(2,1)S(1)} %copy.126, bf16[512,3,32,8,5,1]{0,3,5,4,2,1:T(8,128)(2,1)S(1)} %get-tuple-element.27, bf16[1,32,8,5,128]{4,2,3,1,0:T(8,128)(2,1)S(1)} %fusion.57, ...), kind=kOutput, calls=%fused_computation.36 | convolution fusion | flops 4472799232 | bytes 15663144 | tf_op jit(solution)/shard_map/conv_general_dilated | solution.py:58
  190.5 5.9 %copy.128 = bf16[27,128,512]{2,1,0:T(8,128)(2,1)} copy(bf16[27,128,512]{1,2,0:T(8,128)(2,1)} %bitcast.99) | data formatting | bytes 7077888 | tf_op jit(solution)/shard_map/convert_element_type | solution.py:104
  196.4 2.4 slice.28
  198.8 2.3 copy.100
  201.1 2.3 copy.99
  206.3 4.9 %select_convert_fusion = bf16[1,32,8,5,512]{4,2,3,1,0:T(8,128)(2,1)S(1)} fusion(bf16[3,3,3,128,512]{4,3,2,1,0:T(8,128)(2,1)S(1)} %bitcast.82, bf16[128,3,32,1,7,2]{0,4,5,2,1,3:T(8,128)(2,1)S(1)} %slice.22, bf16[128,3,32,1,8,5]{0,4,5,2,1,3:T(8,128)(2,1)S(1)} %copy.117, pred[8,5]{0,1:T(8,128)(4,1)S(1)} %copy-done.15), kind=kOutput, calls=%fused_computation.34 | convolution fusion | flops 4440915968 | bytes 6176808 | tf_op jit(solution)/shard_map/conv_general_dilated | solution.py:47
  213.7 4.4 %pad_maximum_fusion = bf16[128,1,3,32,32]{0,1,4,3,2:T(2,128)(2,1)S(1)} fusion(bf16[128,1,1,32,32]{0,1,4,3,2:T(2,128)(2,1)} %copy.100, bf16[128,1,1,32,32]{0,1,4,3,2:T(2,128)(2,1)S(1)} %bitcast.93, bf16[128,1,1,32,32]{0,1,4,3,2:T(2,128)(2,1)} %copy.99), kind=kLoop, calls=%fused_computation.40 | loop fusion | flops 786432 | bytes 1572864 | tf_op jit(solution)/shard_map/concatenate | solution.py:18
  218.1 20.5 %convolution_convert_fusion = bf16[3,3,3,128,512]{4,3,2,1,0:T(8,128)(2,1)} fusion(bf16[128,1,3,32,32]{0,1,4,3,2:T(2,128)(2,1)S(1)} %pad_maximum_fusion, bf16[512,1,1,32,32]{0,4,3,2,1:T(8,128)(2,1)} %slice.28), kind=kOutput, calls=%fused_computation.35 | convolution fusion | flops 3476226048 | bytes 5373952 | tf_op jit(solution)/shard_map/conv_general_dilated | solution.py:58
  240.9 5.0 %convolution_select_fusion = f32[1,32,8,5,512]{4,2,3,1,0:T(8,128)S(1)} fusion(bf16[3,3,3,128,512]{4,3,2,1,0:T(8,128)(2,1)S(1)} %bitcast.106, bf16[128,3,32,1,7,2]{0,4,5,2,1,3:T(8,128)(2,1)S(1)} %slice.18, bf16[128,3,32,1,8,5]{0,4,5,2,1,3:T(8,128)(2,1)S(1)} %copy.103, pred[8,5]{0,1:T(8,128)(4,1)S(1)} %copy-done.16), kind=kOutput, calls=%fused_computation.39 | convolution fusion | flops 4440260608 | bytes 7487528 | tf_op jit(solution)/shard_map/conv_general_dilated | solution.py:35
  247.6 2.6 copy.105
  252.2 103.9 %all-reduce.3.cloned.1.call-done = (bf16[27,128,512]{2,1,0:T(8,128)(2,1)}, bf16[27,128,512]{2,1,0:T(8,128)(2,1)}) async-done(((bf16[27,128,512]{2,1,0:T(8,128)(2,1)}, bf16[27,128,512]{2,1,0:T(8,128)(2,1)}), (bf16[27,128,512]{2,1,0:T(8,128)(2,1)}, bf16[27,128,512]{2,1,0:T(8,128)(2,1)})) %all-reduce.3.cloned.1.call-update) | async-done | bytes 7077904 | tf_op jit(solution)/shard_map/psum | solution.py:104
  356.2 6.1 %convert_element_type.52 = f32[27,128,512]{2,1,0:T(8,128)} convert(bf16[27,128,512]{2,1,0:T(8,128)(2,1)} %get-tuple-element.16) | non-fusion elementwise | flops 1769472 | bytes 10616832 | tf_op jit(solution)/shard_map/convert_element_type | solution.py:104
  362.2 4.0 convert_element_type.55
  366.2 35.9 %reduce-scatter.5.cloned.1.call-done = f32[128,1,1,1024]{0,3,2,1:T(8,128)} async-done(((f32[512,1,1,1024]{0,3,2,1:T(8,128)}), f32[128,1,1,1024]{0,3,2,1:T(8,128)}) %reduce-scatter.5.cloned.1.call-update) | async-done | bytes 524304 | tf_op jit(solution)/shard_map/reduce_scatter | solution.py:81
  (97 shorter events, 36.9 us)
Async XLA Ops:
  7.2 83.5 %copy-start = (bf16[27,128,512]{2,1,0:T(8,128)(2,1)S(1)}, bf16[27,128,512]{2,1,0:T(8,128)(2,1)}, u32[]{:S(2)}) copy-start(bf16[27,128,512]{2,1,0:T(8,128)(2,1)} %param.5) | copy-start | bytes 10616836
  7.2 75.6 %all-gather.3.cloned.1.call-start = ((), (), s32[]{:S(2)}) async-start(), calls=%async_computation.2 | async-start | bytes 3932160 | tf_op jit(solution)/shard_map/all_gather | solution.py:75
  9.2 3.7 collective-permute-start
  11.6 3.6 collective-permute-start.1
  17.2 128.8 %all-gather.5.cloned.1.call-start = ((), (), s32[]{:S(2)}) async-start(), calls=%async_computation.4 | async-start | bytes 3932160 | tf_op jit(solution)/shard_map/all_gather | solution.py:88
  19.0 3.4 collective-permute-start.4
  21.1 3.6 collective-permute-start.5
  26.6 223.6 %reduce-scatter.7.cloned.1.call-start = ((), (), s32[]{:S(2)}) async-start(), calls=%async_computation.5 | async-start | bytes 1310720
  88.0 22.3 %copy-start.2 = (bf16[512,3,32,1,40]{0,2,4,1,3:T(8,128)(2,1)}, bf16[512,3,32,1,40]{0,2,4,1,3:T(8,128)(2,1)S(1)}, u32[]{:S(2)}) copy-start(bf16[512,3,32,1,40]{0,2,4,1,3:T(8,128)(2,1)S(1)} %get-tuple-element.22) | copy-start | bytes 11796484
  88.0 2.7 copy-start.15
  101.6 0.8 copy-start.6
  103.1 95.7 %collective-permute-start.3 = (bf16[128,1,1,1024]{0,3,2,1:T(8,128)(2,1)}, bf16[128,1,1,1024]{0,3,2,1:T(8,128)(2,1)}, u32[]{:S(2)}, u32[]{:S(2)}) collective-permute-start(bf16[128,1,1,1024]{0,3,2,1:T(8,128)(2,1)} %bitcast.42), channel_id=1, source_target_pairs={{1,0},{3,2},{5,4},{7,6},{9,8},{11,10},{13,12},{15,14},{17,16},{19,... | collective-permute-start | bytes 786440 | tf_op jit(solution)/shard_map/ppermute | solution.py:17
  104.4 96.7 %collective-permute-start.2 = (bf16[128,1,1,1024]{0,3,2,1:T(8,128)(2,1)}, bf16[128,1,1,1024]{0,3,2,1:T(8,128)(2,1)}, u32[]{:S(2)}, u32[]{:S(2)}) collective-permute-start(bf16[128,1,1,1024]{0,3,2,1:T(8,128)(2,1)} %bitcast.42), channel_id=1, source_target_pairs={{0,1},{2,3},{4,5},{6,7},{8,9},{10,11},{12,13},{14,15},{16,17},{18,... | collective-permute-start | bytes 786440 | tf_op jit(solution)/shard_map/ppermute | solution.py:16
  150.2 2.7 copy-start.13
  150.2 2.7 copy-start.17
  152.9 14.1 %copy-start.5 = (bf16[512,3,32,1,8,4]{0,2,5,4,1,3:T(8,128)(2,1)S(1)}, bf16[512,3,32,1,8,4]{0,2,5,4,1,3:T(8,128)(2,1)}, u32[]{:S(2)}) copy-start(bf16[512,3,32,1,8,4]{0,2,5,4,1,3:T(8,128)(2,1)} %get-tuple-element.18) | copy-start | bytes 9437188
  162.7 4.3 %copy-start.11 = (bf16[128,1,1,32,32]{0,3,4,1,2:T(8,128)(2,1)}, bf16[128,1,1,32,32]{0,3,4,1,2:T(8,128)(2,1)S(1)}, u32[]{:S(2)}) copy-start(bf16[128,1,1,32,32]{0,3,4,1,2:T(8,128)(2,1)S(1)} %slice_bitcast_fusion.2) | copy-start | bytes 786436
  162.7 6.0 %copy-start.4 = (bf16[512,3,32,1,8,4]{0,2,5,4,1,3:T(8,128)(2,1)S(1)}, bf16[512,3,32,1,8,4]{0,2,5,4,1,3:T(8,128)(2,1)}, u32[]{:S(2)}) copy-start(bf16[512,3,32,1,8,4]{0,2,5,4,1,3:T(8,128)(2,1)} %get-tuple-element.19) | copy-start | bytes 9437188
  163.5 40.0 %collective-permute-start.6 = (bf16[128,1,1,1024]{0,3,2,1:T(8,128)(2,1)}, bf16[128,1,1,1024]{0,3,2,1:T(8,128)(2,1)}, u32[]{:S(2)}, u32[]{:S(2)}) collective-permute-start(bf16[128,1,1,1024]{0,3,2,1:T(8,128)(2,1)} %bitcast.20), channel_id=1, source_target_pairs={{0,1},{2,3},{4,5},{6,7},{8,9},{10,11},{12,13},{14,15},{16,17},{18,... | collective-permute-start | bytes 786440 | tf_op jit(solution)/shard_map/ppermute | solution.py:16
  165.6 38.9 %collective-permute-start.7 = (bf16[128,1,1,1024]{0,3,2,1:T(8,128)(2,1)}, bf16[128,1,1,1024]{0,3,2,1:T(8,128)(2,1)}, u32[]{:S(2)}, u32[]{:S(2)}) collective-permute-start(bf16[128,1,1,1024]{0,3,2,1:T(8,128)(2,1)} %bitcast.20), channel_id=1, source_target_pairs={{1,0},{3,2},{5,4},{7,6},{9,8},{11,10},{13,12},{15,14},{17,16},{19,... | collective-permute-start | bytes 786440 | tf_op jit(solution)/shard_map/ppermute | solution.py:17
  168.7 1.8 copy-start.10
  168.7 2.2 copy-start.9
  168.7 2.6 copy-start.3
  196.4 9.2 %copy-start.12 = (bf16[128,1,1,32,32]{0,3,4,1,2:T(8,128)(2,1)S(1)}, bf16[128,1,1,32,32]{0,3,4,1,2:T(8,128)(2,1)}, u32[]{:S(2)}) copy-start(bf16[128,1,1,32,32]{0,3,4,1,2:T(8,128)(2,1)} %copy-done.11) | copy-start | bytes 786436
  211.6 2.1 copy-start.7
  213.7 142.5 %all-reduce.3.cloned.1.call-start = ((), (), s32[]{:S(2)}) async-start(), calls=%async_computation.6 | async-start | bytes 14155776 | tf_op jit(solution)/shard_map/psum | solution.py:104
  238.7 163.4 %reduce-scatter.5.cloned.1.call-start = ((), (), s32[]{:S(2)}) async-start(), calls=%async_computation.3 | async-start | bytes 2621440 | tf_op jit(solution)/shard_map/reduce_scatter | solution.py:81
  238.9 2.0 copy-start.14
  238.9 2.0 copy-start.16
  356.2 6.1 %copy-start.8 = (bf16[27,128,512]{2,1,0:T(8,128)(2,1)S(1)}, bf16[27,128,512]{2,1,0:T(8,128)(2,1)}, u32[]{:S(2)}) copy-start(bf16[27,128,512]{2,1,0:T(8,128)(2,1)} %get-tuple-element.17) | copy-start | bytes 10616836
  362.2 43.4 %copy-start.1 = (bf16[27,128,512]{2,1,0:T(8,128)(2,1)S(1)}, bf16[27,128,512]{2,1,0:T(8,128)(2,1)}, u32[]{:S(2)}) copy-start(bf16[27,128,512]{2,1,0:T(8,128)(2,1)} %param.5) | copy-start | bytes 10616836
Sparse Core Ops, SparseCore 0:
  17.3 65.4 all-gather.2
  84.3 61.5 all-gather.4
  213.8 27.3 reduce-scatter.6
  245.0 111.0 all-reduce.2
  358.3 43.7 reduce-scatter.4
where the time goes:
time: 416 us; the launch traced here: 413 us
  waiting for transfers between devices  233 us (56%)
  matrix products  65.8 us (16%)
  local copies, waits for them, and re-layouts  61.1 us (15%)
  other arithmetic  21.6 us (5%)
  starting transfers between devices  16.5 us (4%)
  between operations  14.8 us (4%)
    psum x1, waiting for transfers between devices, body(): lax.psum(local_one.astype(jnp.bfloat16), ('samples', 'spatial'))  104 us
    all_gather x1, waiting for transfers between devices, body(): whole_x = lax.all_gather(rims_x, 'channel', axis=0, tiled=True)  56.1 us
    conv_general_dilated x2, matrix products, weight_grad(): lax.conv_general_dilated(padded, upstream, (1, 1, 1), [(0, 0), (0, 0), (0...  36 us
    reduce_scatter x1, waiting for transfers between devices, body(): lax.psum_scatter(to_flat(forward_conv(grid_h, weight_part, 'DHWIO')), 'ch...  35.9 us
    all_gather x1, waiting for transfers between devices, body(): whole_c = to_grid(lax.all_gather(rims_c, 'channel', axis=0, tiled=True))  32.2 us
    unnamed x52, local copies, waits for them, and re-layouts  24.2 us
    conv_general_dilated x2, matrix products, forward_conv(): lax.conv_general_dilated(source, as_taps(kernel), (1, 1, 1), [(0, 0), (1,...  15.2 us
    conv_general_dilated x2, matrix products, data_grad(): lax.conv_general_dilated(source, flipped, (1, 1, 1), [(0, 0), (1, 1), (1,...  14.6 us
  transfers between devices with their start and end apart: 13, of which 6 were waited for; matrix products, arithmetic and copies ran while one was open for 32% of the time, Pallas kernels for 0%

commit v1 on v0

--- a/solution.py
+++ b/solution.py
@@ -101,7 +101,9 @@
     local_two = weight_grad(pad_plane(grid_h), whole_c[:, :, 1:-1], "DHWNC")
     local_one = weight_grad(pad_plane(to_grid(whole_x)), act_grad, "DHWCN")
     grad_one, grad_two = (
-        lax.psum(local_one.astype(jnp.bfloat16), ("samples", "spatial")).astype(jnp.float32),
+        jnp.sum(
+            lax.all_gather(local_one.astype(jnp.bfloat16), ("samples", "spatial")), axis=0
+        ).astype(jnp.float32),
         lax.psum(local_two.astype(jnp.bfloat16), ("samples", "spatial")).astype(jnp.float32),
     )
     return (mixed_out, input_grad, grad_one, grad_two)

time: 416 us -> 519 us (1.25)
  waiting for transfers between devices: 233 us -> 305 us
  local copies, waits for them, and re-layouts: 61.1 us -> 81.2 us
  other arithmetic: 21.6 us -> 31.6 us
    all_gather x0 -> x1, waiting for transfers between devices: none -> 136 us  [body(): lax.all_gather(local_one.astype(jnp.bfloat16), ('samples', 'spatial'))]
    psum x1, waiting for transfers between devices: 104 us -> 4.55 us  [body(): lax.psum(local_two.astype(jnp.bfloat16), ('samples', 'spatial'))]
    unnamed x6 -> x7, waiting for transfers between devices: 0.1 us -> 23.7 us
    unnamed x52 -> x50, local copies, waits for them, and re-layouts: 24.2 us -> 42.5 us
    reduce_sum x0 -> x1, other arithmetic: none -> 13.1 us  [body(): jnp.sum(lax.all_gather(local_one.astype(jnp.bfloat16), ('samples', 'spati...]
    all_gather x1, waiting for transfers between devices: 32.2 us -> 38.6 us  [body(): whole_c = to_grid(lax.all_gather(rims_c, 'channel', axis=0, tiled=True))]
    convert_element_type x1 -> x0, other arithmetic: 6.08 us -> none  [body(): lax.psum(local_one.astype(jnp.bfloat16), ('samples', 'spatial'))]
  transfers between devices with their start and end apart: 13 -> 14, of which waited for: 6 -> 8; matrix products, arithmetic and copies ran while one was open for 32% -> 29% of each run, Pallas kernels for 0% -> 0%
where the time goes in v1:
time: 519 us; the launch traced here: 515 us
  waiting for transfers between devices  305 us (59%)
  local copies, waits for them, and re-layouts  81.2 us (16%)
  matrix products  68 us (13%)
  other arithmetic  31.6 us (6%)
  between operations  14.8 us (3%)
  starting transfers between devices  14.7 us (3%)
    all_gather x1, waiting for transfers between devices, body(): lax.all_gather(local_one.astype(jnp.bfloat16), ('samples', 'spatial'))  136 us
    all_gather x1, waiting for transfers between devices, body(): whole_x = lax.all_gather(rims_x, 'channel', axis=0, tiled=True)  56.1 us
    unnamed x50, local copies, waits for them, and re-layouts  42.5 us
    reduce_scatter x1, waiting for transfers between devices, body(): lax.psum_scatter(to_flat(forward_conv(grid_h, weight_part, 'DHWIO')), 'ch...  40.7 us
    all_gather x1, waiting for transfers between devices, body(): whole_c = to_grid(lax.all_gather(rims_c, 'channel', axis=0, tiled=True))  38.6 us
    conv_general_dilated x2, matrix products, weight_grad(): lax.conv_general_dilated(padded, upstream, (1, 1, 1), [(0, 0), (0, 0), (0...  38.2 us
    unnamed x7, waiting for transfers between devices  23.7 us
    conv_general_dilated x2, matrix products, forward_conv(): lax.conv_general_dilated(source, as_taps(kernel), (1, 1, 1), [(0, 0), (1,...  15.2 us
  transfers between devices with their start and end apart: 14, of which 8 were waited for; matrix products, arithmetic and copies ran while one was open for 29% of the time, Pallas kernels for 0%

profile of v1, /device:TPU:0, one launch (start us, length us, event | category | flops | bytes accessed | tf_op | source)
XLA Modules:
  0.0 515.2 jit_solution(11159752465681486901)
XLA Ops:
  9.2 2.4 collective-permute-start
  12.9 2.3 collective-permute-done.1
  22.4 2.3 collective-permute-done.5
  26.7 56.1 %all-gather.4.cloned.1.call-done = bf16[512,1,3,1024]{0,3,2,1:T(8,128)(2,1)} async-done(((bf16[128,1,3,1024]{0,3,2,1:T(8,128)(2,1)}), bf16[512,1,3,1024]{0,3,2,1:T(8,128)(2,1)}) %all-gather.4.cloned.1.call-update) | async-done | bytes 3145744 | tf_op jit(solution)/shard_map/all_gather | solution.py:75
  82.8 3.6 copy.144
  86.4 2.9 fusion.85
  92.0 10.3 %multiply_convert_fusion = (bf16[1,32,8,5,128]{4,2,3,1,0:T(8,128)(2,1)S(1)}, f32[1,32,8,5,128]{4,2,3,1,0:T(8,128)}) fusion(bf16[3,3,3,128,512]{4,3,2,1,0:T(8,128)(2,1)S(1)} %bitcast.81, bf16[512,3,32,1,7,2]{0,4,5,2,1,3:T(8,128)(2,1)S(1)} %slice.16, bf16[512,3,32,1,8,5]{0,4,5,2,1,3:T(8,128)(2,1)S(1)} %copy.93, pred[8,5]{0,1:T(8,128)(4,1)S(1)} %copy-done.13), kind=kOutput, calls=%fused_computation.63 | convolution fusion | flops 4452974592 | bytes 9830440 | tf_op jit(solution)/shard_map/conv_general_dilated | solution.py:35
  107.9 38.6 %all-gather.6.cloned.1.call-done = bf16[512,1,3,1024]{0,3,2,1:T(8,128)(2,1)} async-done(((bf16[128,1,3,1024]{0,3,2,1:T(8,128)(2,1)}), bf16[512,1,3,1024]{0,3,2,1:T(8,128)(2,1)}) %all-gather.6.cloned.1.call-update) | async-done | bytes 3145744 | tf_op jit(solution)/shard_map/all_gather | solution.py:88
  146.5 3.6 copy.146
  150.7 2.2 copy.108
  153.4 9.6 %fusion.57 = bf16[1,32,8,5,128]{4,2,3,1,0:T(8,128)(2,1)S(1)} fusion(bf16[3,3,3,128,512]{4,3,2,1,0:T(8,128)(2,1)S(1)} %bitcast.105, bf16[512,3,32,1,7,2]{0,4,5,2,1,3:T(8,128)(2,1)S(1)} %slice.20, bf16[512,3,32,1,8,5]{0,4,5,2,1,3:T(8,128)(2,1)S(1)} %copy.108, f32[1,32,8,5,128]{4,2,3,1,0:T(8,128)S(1)} %copy-done.15, pred[8,5]{0,1:T(8,128)(4,1)S(1)} %copy-done.13), kind=kOutput, calls=%fused_computation.54 | convolution fusion | flops 4453629952 | bytes 9830440 | tf_op jit(solution)/shard_map/conv_general_dilated | solution.py:47
  172.4 3.1 pad_maximum_fusion
  175.5 20.2 %convolution_convert_fusion = bf16[3,3,3,128,512]{4,3,2,1,0:T(8,128)(2,1)} fusion(bf16[128,1,3,32,32]{0,1,4,3,2:T(2,128)(2,1)S(1)} %pad_maximum_fusion, bf16[512,1,1,32,32]{0,4,3,2,1:T(8,128)(2,1)S(1)} %slice.28), kind=kOutput, calls=%fused_computation.35 | convolution fusion | flops 3476226048 | bytes 5373952 | tf_op jit(solution)/shard_map/conv_general_dilated | solution.py:58
  196.2 3.4 fusion.83
  199.6 3.4 copy.140
  203.0 3.4 copy.141
  209.3 4.9 select_convert_fusion
  216.3 2.3 copy.133
  221.4 4.1 copy.123
  225.5 3.8 fusion.25
  231.5 4.9 convolution_select_fusion
  238.2 2.6 copy.102
  241.1 18.1 %fusion.32 = bf16[3,3,3,128,512,1]{3,4,2,5,1,0:T(8,128)(2,1)} fusion(bf16[512,3,32,8,5,1]{0,3,5,4,2,1:T(8,128)(2,1)} %get-tuple-element.24, bf16[512,3,32,8,5,1]{0,3,5,4,2,1:T(8,128)(2,1)} %copy.123, bf16[512,3,32,8,5,1]{0,3,5,4,2,1:T(8,128)(2,1)} %get-tuple-element.25, bf16[1,32,8,5,128]{4,2,3,1,0:T(8,128)(2,1)} %copy-done.10, pred[8,5]{0,1:T(8,128)(4,1)S(1)} %copy-done.14), kind=kOutput, calls=%fused_computation.36 | convolution fusion | flops 4472799232 | bytes 15663144 | tf_op jit(solution)/shard_map/conv_general_dilated | solution.py:58
  259.2 5.8 %copy.125 = bf16[1,27,128,512]{3,2,1,0:T(8,128)(2,1)} copy(bf16[1,27,128,512]{2,3,1,0:T(8,128)(2,1)} %bitcast.99) | data formatting | bytes 7077888 | tf_op jit(solution)/shard_map/convert_element_type | solution.py:105
  265.0 4.5 all-reduce.2.cloned.1.call-done
  269.6 5.9 %convert_element_type.64 = f32[27,128,512]{2,1,0:T(8,128)} convert(bf16[27,128,512]{2,1,0:T(8,128)(2,1)} %all-reduce.2.cloned.1.call-done) | non-fusion elementwise | flops 1769472 | bytes 10616832 | tf_op jit(solution)/shard_map/convert_element_type | solution.py:107
  275.5 23.6 %reduce-scatter.7.cloned.1.call-done = bf16[128,1024]{1,0:T(8,128)(2,1)} async-done(((bf16[512,1024]{1,0:T(8,128)(2,1)}), bf16[128,1024]{1,0:T(8,128)(2,1)}) %reduce-scatter.7.cloned.1.call-update) | async-done | bytes 262160
  302.7 40.7 %reduce-scatter.5.cloned.1.call-done = f32[128,1,1,1024]{0,3,2,1:T(8,128)} async-done(((f32[512,1,1,1024]{0,3,2,1:T(8,128)}), f32[128,1,1,1024]{0,3,2,1:T(8,128)}) %reduce-scatter.5.cloned.1.call-update) | async-done | bytes 524304 | tf_op jit(solution)/shard_map/reduce_scatter | solution.py:81
  347.0 136.5 %all-gather.8.cloned.1.call-done = bf16[8,27,128,512]{3,2,1,0:T(8,128)(2,1)} async-done(((bf16[1,27,128,512]{3,2,1,0:T(8,128)(2,1)}), bf16[8,27,128,512]{3,2,1,0:T(8,128)(2,1)}) %all-gather.8.cloned.1.call-update) | async-done | bytes 28311568 | tf_op jit(solution)/shard_map/all_gather | solution.py:105
  483.4 13.1 %reduce_sum.12 = bf16[27,128,512]{2,1,0:T(8,128)(2,1)} reduce(bf16[8,27,128,512]{3,2,1,0:T(8,128)(2,1)} %all-gather.8.cloned.1.call-done, bf16[]{:T(256)} %constant.8.clone.1), dimensions={0}, to_apply=%region_2.3 | reduce | flops 12386304 | bytes 31850498 | tf_op jit(solution)/shard_map/reduce_sum | solution.py:104
  496.5 5.7 %copy.137 = bf16[27,128,512]{1,2,0:T(8,128)(2,1)} copy(bf16[27,128,512]{2,1,0:T(8,128)(2,1)} %reduce_sum.12) | data formatting | bytes 7077888
  502.3 5.9 %copy.130 = f32[27,128,512]{2,1,0:T(8,128)} copy(bf16[27,128,512]{1,2,0:T(8,128)(2,1)} %copy.137) | data formatting | bytes 10616832
  (98 shorter events, 50.2 us)
Async XLA Ops:
  7.2 84.8 %copy-start = (bf16[27,128,512]{2,1,0:T(8,128)(2,1)S(1)}, bf16[27,128,512]{2,1,0:T(8,128)(2,1)}, u32[]{:S(2)}) copy-start(bf16[27,128,512]{2,1,0:T(8,128)(2,1)} %param.5) | copy-start | bytes 10616836
  7.2 75.6 %all-gather.4.cloned.1.call-start = ((), (), s32[]{:S(2)}) async-start(), calls=%async_computation.2 | async-start | bytes 3932160 | tf_op jit(solution)/shard_map/all_gather | solution.py:75
  9.2 3.7 collective-permute-start
  11.6 3.6 collective-permute-start.1
  17.2 129.4 %all-gather.6.cloned.1.call-start = ((), (), s32[]{:S(2)}) async-start(), calls=%async_computation.4 | async-start | bytes 3932160 | tf_op jit(solution)/shard_map/all_gather | solution.py:88
  19.0 3.4 collective-permute-start.4
  21.0 3.6 collective-permute-start.5
  26.6 242.9 %all-reduce.2.cloned.1.call-start = ((), (), s32[]{:S(2)}) async-start(), calls=%async_computation.6 | async-start | bytes 7077888 | tf_op jit(solution)/shard_map/psum | solution.py:107
  89.3 2.7 copy-start.13
  102.9 0.8 copy-start.6
  104.4 64.9 %collective-permute-start.2 = (bf16[128,1,1,1024]{0,3,2,1:T(8,128)(2,1)}, bf16[128,1,1,1024]{0,3,2,1:T(8,128)(2,1)}, u32[]{:S(2)}, u32[]{:S(2)}) collective-permute-start(bf16[128,1,1,1024]{0,3,2,1:T(8,128)(2,1)} %bitcast.42), channel_id=1, source_target_pairs={{0,1},{2,3},{4,5},{6,7},{8,9},{10,11},{12,13},{14,15},{16,17},{18,... | collective-permute-start | bytes 786440 | tf_op jit(solution)/shard_map/ppermute | solution.py:16
  106.4 64.4 %collective-permute-start.3 = (bf16[128,1,1,1024]{0,3,2,1:T(8,128)(2,1)}, bf16[128,1,1,1024]{0,3,2,1:T(8,128)(2,1)}, u32[]{:S(2)}, u32[]{:S(2)}) collective-permute-start(bf16[128,1,1,1024]{0,3,2,1:T(8,128)(2,1)} %bitcast.42), channel_id=1, source_target_pairs={{1,0},{3,2},{5,4},{7,6},{9,8},{11,10},{13,12},{15,14},{17,16},{19,... | collective-permute-start | bytes 786440 | tf_op jit(solution)/shard_map/ppermute | solution.py:17
  150.7 2.7 copy-start.11
  150.7 2.7 copy-start.15
  163.1 7.7 %copy-start.10 = (bf16[1,32,8,5,128]{4,2,3,1,0:T(8,128)(2,1)}, bf16[1,32,8,5,128]{4,2,3,1,0:T(8,128)(2,1)S(1)}, u32[]{:S(2)}) copy-start(bf16[1,32,8,5,128]{4,2,3,1,0:T(8,128)(2,1)S(1)} %fusion.57) | copy-start | bytes 983044
  163.1 9.3 %copy-start.7 = (bf16[1,32,1,32,128]{4,2,3,1,0:T(2,128)(2,1)S(1)}, bf16[1,32,1,32,128]{4,2,3,1,0:T(2,128)(2,1)}, u32[]{:S(2)}) copy-start(bf16[1,32,1,32,128]{4,2,3,1,0:T(2,128)(2,1)} %copy-done.6) | copy-start | bytes 786436
  163.2 0.7 copy-start.8
  164.7 41.8 %collective-permute-start.6 = (bf16[128,1,1,1024]{0,3,2,1:T(8,128)(2,1)}, bf16[128,1,1,1024]{0,3,2,1:T(8,128)(2,1)}, u32[]{:S(2)}, u32[]{:S(2)}) collective-permute-start(bf16[128,1,1,1024]{0,3,2,1:T(8,128)(2,1)} %bitcast.20), channel_id=1, source_target_pairs={{0,1},{2,3},{4,5},{6,7},{8,9},{10,11},{12,13},{14,15},{16,17},{18,... | collective-permute-start | bytes 786440 | tf_op jit(solution)/shard_map/ppermute | solution.py:16
  166.7 40.9 %collective-permute-start.7 = (bf16[128,1,1,1024]{0,3,2,1:T(8,128)(2,1)}, bf16[128,1,1,1024]{0,3,2,1:T(8,128)(2,1)}, u32[]{:S(2)}, u32[]{:S(2)}) collective-permute-start(bf16[128,1,1,1024]{0,3,2,1:T(8,128)(2,1)} %bitcast.20), channel_id=1, source_target_pairs={{1,0},{3,2},{5,4},{7,6},{9,8},{11,10},{13,12},{15,14},{17,16},{19,... | collective-permute-start | bytes 786440 | tf_op jit(solution)/shard_map/ppermute | solution.py:17
  175.5 20.2 %copy-start.4 = (bf16[128,1,3,32,32]{0,1,4,3,2:T(2,128)(2,1)}, bf16[128,1,3,32,32]{0,1,4,3,2:T(2,128)(2,1)S(1)}, u32[]{:S(2)}) copy-start(bf16[128,1,3,32,32]{0,1,4,3,2:T(2,128)(2,1)S(1)} %pad_maximum_fusion) | copy-start | bytes 2359300
  195.7 103.4 %reduce-scatter.7.cloned.1.call-start = ((), (), s32[]{:S(2)}) async-start(), calls=%async_computation.7 | async-start | bytes 1310720
  203.0 5.6 %copy-start.9 = (bf16[128,1,1,32,32]{0,3,4,1,2:T(8,128)(2,1)S(1)}, bf16[128,1,1,32,32]{0,3,4,1,2:T(8,128)(2,1)}, u32[]{:S(2)}) copy-start(bf16[128,1,1,32,32]{0,3,4,1,2:T(8,128)(2,1)} %copy-done.8) | copy-start | bytes 786436
  206.5 2.9 copy-start.14
  218.6 124.8 %reduce-scatter.5.cloned.1.call-start = ((), (), s32[]{:S(2)}) async-start(), calls=%async_computation.3 | async-start | bytes 2621440 | tf_op jit(solution)/shard_map/reduce_scatter | solution.py:81
  218.9 2.5 copy-start.1
  221.4 4.1 copy-start.2
  221.4 4.1 copy-start.3
  225.5 3.8 copy-start.5
  229.5 2.0 copy-start.12
  240.9 242.5 %all-gather.8.cloned.1.call-start = ((), (), s32[]{:S(2)}) async-start(), calls=%async_computation.5 | async-start | bytes 31850496 | tf_op jit(solution)/shard_map/all_gather | solution.py:105
Sparse Core Ops, SparseCore 0:
  17.3 65.4 all-gather.3
  84.9 61.5 all-gather.5
  195.8 73.7 all-reduce.1
  271.7 27.3 reduce-scatter.6
  301.2 42.1 reduce-scatter.4
  345.7 137.6 all-gather.7
